TPU v7x, 256 devices: a whole 4x4x8 slice. The times are simulated.
256 devices in a mesh: tok: 16 (over y_lo, x, core), mdl: 16 (over y_hi, z).
Axes of the slice: x: 4, y: 4 (y_hi: 2, y_lo: 2; y = y_hi * 2 + y_lo), z: 8, core: 2. Of those that a mesh axis runs over, the one named last changes fastest.
Arguments:
- hidden: bfloat16 [8192, 2048], P('tok'), may hold values from -40 to 40
- segment_ids: int32 [8192], replicated, may hold values from 0 to 3, never falling along the last dimension, each value on 1 to 4096 neighbouring positions
- routes: int32 [8192, 2], P('tok'), may hold values from 0 to 7, all different within a row; in each aligned block of 512 rows (0 to 511, 512 to 1023, ...) at most 256 rows name the same one
- norm_gain: float32 [2048], replicated, may hold values from 0.5 to 1.5
- router_weight: float32 [2048, 8], replicated, may hold values from -0.125 to 0.125
- query_weight: bfloat16 [8, 2048, 2048], P(None, 'tok', 'mdl'), may hold values from -2 to 2
- kv_weight: bfloat16 [2, 2048, 2048], P(None, 'tok', 'mdl'), may hold values from -16 to 16
- out_weight: bfloat16 [8, 2048, 2048], P(None, 'mdl', 'tok'), may hold values from -0.5 to 0.5
- page_table: int32 [512], P('tok'), may hold values from 0 to 511, as said below
Outputs:
- output: bfloat16 [8192, 2048], P('tok', 'mdl')
- cache: bfloat16 [512, 16, 2, 2048], P('tok', None, None, 'mdl')
Inputs may be any that keep to these rules, and one draw needn't show every extreme that they name: `segment_ids`: Non-decreasing along the tokens; every prompt number 0 to 3 occurs, each prompt 1 to 4096 tokens long, one exactly 4096. `routes`: each token names 2 different experts; among the 512 tokens of an aligned block no expert is named more than 256 times, and some block reaches 256. `page_table`: A permutation of the 512 physical pages; of the 32 logical pages of each aligned block, exactly 2 lie in each aligned range of 32 physical pages.
All inputs are finite; a program needn't handle non-finite values.
Results may differ from a plain program's by a relative error of at most 0.019.
Values may be sent and summed in bfloat16 or wider, within the bound.
No kernel may reach another device: no remote copies, remote signals or barrier semaphores. Data moves between devices by JAX's collectives and lax.ppermute only.
A program may use at most 128 MiB of HBM per device.

v0:
```python
import math
import jax
import jax.numpy as jnp
from jax import lax
from jax.sharding import PartitionSpec as P

HDIM = 128
SEGS = 4
EPSILON = 1e-05
MASKED = -1e30


def rms_norm(hidden, norm_gain):
    values = hidden.astype(jnp.float32)
    factor = lax.rsqrt(jnp.mean(values * values, axis=-1, keepdims=True) + EPSILON)
    return (values * factor * norm_gain).astype(jnp.bfloat16)


def route_gates(normed, router_weight, routes):
    logits = jnp.dot(normed.astype(jnp.float32), router_weight, precision=lax.Precision.HIGHEST)
    expert_ids = jnp.arange(logits.shape[1], dtype=jnp.int32)
    picked = routes[:, :, None] == expert_ids[None, None, :]
    chosen = jnp.sum(jnp.where(picked, logits[:, None, :], jnp.float32(0.0)), axis=-1)
    return jax.nn.softmax(chosen, axis=-1)


def place_pages(key_values, page_table, shards, tok_row):
    pages_here = page_table.shape[0]
    per_peer = pages_here // shards
    page_rows = key_values.shape[0] // pages_here
    head_cols = key_values.shape[2]
    targets = page_table // pages_here
    onehot = (targets[:, None] == jnp.arange(shards, dtype=jnp.int32)[None, :]).astype(jnp.int32)
    ranks = jnp.sum((jnp.cumsum(onehot, axis=0) - 1) * onehot, axis=1)
    ordering = (
        jnp.zeros((pages_here,), jnp.int32)
        .at[targets * per_peer + ranks]
        .set(jnp.arange(pages_here, dtype=jnp.int32))
    )
    outgoing = key_values.reshape(pages_here, page_rows, 2, head_cols)[ordering].reshape(
        shards, per_peer, page_rows, 2, head_cols
    )
    labels = page_table[ordering].reshape(shards, per_peer)
    incoming, got_labels = (
        lax.all_to_all(outgoing, "tok", split_axis=0, concat_axis=0, tiled=True),
        lax.all_to_all(labels, "tok", split_axis=0, concat_axis=0, tiled=True),
    )
    places = got_labels.reshape(-1) - tok_row * pages_here
    arrived = incoming.reshape(pages_here, page_rows, 2, head_cols)
    return jnp.zeros((pages_here, page_rows, 2, head_cols), jnp.bfloat16).at[places].set(arrived)


def local(
    hidden,
    segment_ids,
    routes,
    norm_gain,
    router_weight,
    query_weight,
    kv_weight,
    out_weight,
    page_table,
):
    tok_dev, width = hidden.shape
    experts = query_weight.shape[0]
    head_cols = query_weight.shape[2]
    heads_here = head_cols // HDIM
    capacity = tok_dev // 2
    top_count = routes.shape[1]
    assigned = tok_dev * top_count
    shards = lax.axis_size("tok")
    tok_row = lax.axis_index("tok")
    normed = rms_norm(hidden, norm_gain)
    gates = route_gates(normed, router_weight, routes)
    flat_expert = routes.reshape(-1)
    expert_ids = jnp.arange(experts, dtype=jnp.int32)
    onehot = (flat_expert[:, None] == expert_ids[None, :]).astype(jnp.int32)
    ranks = jnp.sum((jnp.cumsum(onehot, axis=0) - 1) * onehot, axis=1)
    slots = flat_expert * capacity + ranks
    assign_ids = jnp.arange(assigned, dtype=jnp.int32)
    slot_assign = jnp.zeros((experts * capacity,), jnp.int32).at[slots].set(assign_ids)
    slot_token = slot_assign // top_count
    slot_filled = jnp.zeros((experts * capacity,), jnp.bfloat16).at[slots].set(jnp.bfloat16(1.0))
    slot_gate = jnp.zeros((experts * capacity,), jnp.float32).at[slots].set(gates.reshape(-1))
    grouped = (normed[slot_token] * slot_filled[:, None]).reshape(experts, capacity, width)
    query_part = lax.all_gather(query_weight, "tok", axis=1, tiled=True)
    key_part = lax.all_gather(kv_weight, "tok", axis=1, tiled=True)
    query_total = jnp.einsum(
        "ecd,edh->ech", grouped, query_part, preferred_element_type=jnp.float32
    )
    key_total = jnp.einsum("td,kdh->tkh", normed, key_part, preferred_element_type=jnp.float32)
    queries = query_total.astype(jnp.bfloat16).reshape(experts * capacity, head_cols)[slots]
    key_values = key_total.astype(jnp.bfloat16)
    cache = place_pages(key_values, page_table, shards, tok_row)
    by_head_q = queries.reshape(assigned, heads_here, HDIM).transpose(1, 0, 2)
    q_pos = tok_row * tok_dev + assign_ids // top_count
    q_seg = segment_ids[q_pos]
    prompt_ids = jnp.arange(SEGS, dtype=jnp.int32)
    seg_first = jnp.sum((segment_ids[:, None] < prompt_ids[None, :]).astype(jnp.int32), axis=0)
    q_lower = jnp.sum(
        jnp.where(q_seg[:, None] == prompt_ids[None, :], seg_first[None, :], 0), axis=1
    )
    start_state = (
        jnp.full((heads_here, assigned), MASKED, jnp.float32),
        jnp.zeros((heads_here, assigned), jnp.float32),
        jnp.zeros((heads_here, assigned, HDIM), jnp.float32),
    )
    state = start_state
    piece = lax.all_gather(key_values, "tok", axis=0, tiled=True)
    count = piece.shape[0]
    block = math.gcd(count, 512)
    key_blocks = piece[:, 0].reshape(count // block, block, heads_here, HDIM)
    value_blocks = piece[:, 1].reshape(count // block, block, heads_here, HDIM)
    firsts = block * jnp.arange(count // block, dtype=jnp.int32)

    def one_block(carry, inputs):
        peak, total, accum = carry
        key_block, value_block, first = inputs
        k_pos = first + jnp.arange(block, dtype=jnp.int32)
        allowed = (k_pos[None, :] >= q_lower[:, None]) & (k_pos[None, :] <= q_pos[:, None])
        scores = jnp.einsum(
            "hqd,khd->hqk", by_head_q, key_block, preferred_element_type=jnp.float32
        ) / math.sqrt(HDIM)
        scores = jnp.where(allowed[None], scores, jnp.float32(MASKED))
        new_peak = jnp.maximum(peak, jnp.max(scores, axis=-1))
        shrink = jnp.exp(peak - new_peak)
        expon = jnp.where(allowed[None], jnp.exp(scores - new_peak[..., None]), jnp.float32(0.0))
        total = total * shrink + jnp.sum(expon, axis=-1)
        accum = accum * shrink[..., None] + jnp.einsum(
            "hqk,khd->hqd",
            expon.astype(jnp.bfloat16),
            value_block,
            preferred_element_type=jnp.float32,
        )
        return ((new_peak, total, accum), None)

    state, _ = lax.scan(one_block, state, (key_blocks, value_blocks, firsts))
    attended = (
        (state[2] / state[1][..., None])
        .astype(jnp.bfloat16)
        .transpose(1, 0, 2)
        .reshape(assigned, head_cols)
    )
    grouped_out = (attended[slot_assign] * slot_filled[:, None]).reshape(
        experts, capacity, head_cols
    )
    piece = lax.all_gather(out_weight, "tok", axis=2, tiled=True)
    count = piece.shape[2]
    terms = jnp.einsum(
        "ech,ehn->ecn", grouped_out, piece, preferred_element_type=jnp.float32
    ).reshape(experts * capacity, count)
    partial_sums = (
        jnp.zeros((tok_dev, count), jnp.float32).at[slot_token].add(terms * slot_gate[:, None])
    )
    mine = lax.psum_scatter(
        partial_sums.astype(jnp.bfloat16), "mdl", scatter_dimension=1, tiled=True
    ).astype(jnp.float32)
    span = width // lax.axis_size("mdl")
    residual_part = lax.dynamic_slice_in_dim(hidden, lax.axis_index("mdl") * span, span, 1)
    output = (residual_part.astype(jnp.float32) + mine).astype(jnp.bfloat16)
    return (output, cache)


def solution(mesh):
    placed = (
        P("tok", None),
        P(),
        P("tok", None),
        P(),
        P(),
        P(None, "tok", "mdl"),
        P(None, "tok", "mdl"),
        P(None, "mdl", "tok"),
        P("tok"),
    )
    return jax.shard_map(
        local,
        mesh=mesh,
        in_specs=placed,
        out_specs=(P("tok", "mdl"), P("tok", None, None, "mdl")),
        check_vma=False,
    )
```

profile of v0, /device:TPU:4, one launch (start us, length us, event | category | flops | bytes accessed | tf_op | source)
XLA Modules:
  0.0 475.9 jit_solution(12940662665245141497)
XLA Ops:
  11.6 35.2 %all-gather.5.cloned.1.call-done = bf16[2,2048,128]{2,1,0:T(8,128)(2,1)} async-done(((bf16[2,128,128]{2,1,0:T(8,128)(2,1)}), bf16[2,2048,128]{2,1,0:T(8,128)(2,1)}) %all-gather.5.cloned.1.call-update) | async-done | bytes 1048592 | tf_op jit(solution)/shard_map/all_gather | solution.py:87
  46.8 2.6 fusion.45
  50.9 6.2 %gather_fusion = s32[1024]{0:T(1024)S(1)} fusion(s32[8192]{0:T(1024)S(1)} %copy-done.2, s32[1024]{0:T(1024)S(1)} %broadcast_clamp_fusion.2), kind=kCustom, calls=%fused_computation | custom fusion | bytes 12288 | tf_op jit(solution)/shard_map/gather | solution.py:97
  57.4 2.3 reduce-window.6
  60.2 7.6 %scatter_custom_fusion.1 = bf16[2048]{0:T(1024)(128)(2,1)S(1)} fusion(s32[1024]{0:T(1024)S(1)} %bitcast.131, bf16[1024]{0:T(1024)(128)(2,1)S(1)} %broadcast.244, bf16[]{:T(256)} %constant.112.clone.1), kind=kCustom, calls=%fused_computation.125 | custom fusion | bytes 4098 | tf_op jit(solution)/shard_map/scatter | solution.py:83
  67.9 4.3 scatter_custom_fusion
  74.4 11.0 %gather_fusion.1 = bf16[2048,2048]{1,0:T(8,128)(2,1)} fusion(bf16[512,2048]{1,0:T(8,128)(2,1)S(1)} %fusion.36, s32[2048]{0:T(1024)S(1)} %get-tuple-element.163), kind=kCustom, calls=%fused_computation.1 | custom fusion | bytes 16785408 | tf_op jit(solution)/shard_map/gather | solution.py:85
  85.5 4.5 scatter_custom_fusion.2
  90.0 7.0 %fusion.42 = bf16[8,256,128]{2,1,0:T(8,128)(2,1)S(1)} fusion(bf16[8,2048,128]{2,1,0:T(8,128)(2,1)} %all-gather.9.cloned.1.call-done, bf16[8,256,2048]{2,1,0:T(8,128)(2,1)} %bitcast.113, bf16[8,256]{1,0:T(8,128)(2,1)S(1)} %mul.112), kind=kOutput, calls=%fused_computation.68 | convolution fusion | flops 1078198272 | bytes 13111296 | tf_op jit(solution)/shard_map/ecd,edh->ech/dot_general | solution.py:88
  97.0 3.2 gather_fusion.2
  100.2 30.9 %all-gather.7.cloned.1.call-done = bf16[8192,2,128]{2,0,1:T(8,128)(2,1)} async-done(((bf16[512,2,128]{2,0,1:T(8,128)(2,1)}), bf16[8192,2,128]{2,0,1:T(8,128)(2,1)}) %all-gather.7.cloned.1.call-update) | async-done | bytes 4194320 | tf_op jit(solution)/shard_map/all_gather | solution.py:109
  131.1 3.8 fusion.71
  134.9 73.6 %while.15 = (s32[]{:T(128)}, f32[1,1024]{1,0:T(1,128)S(1)}, f32[1,1024]{1,0:T(1,128)S(1)}, f32[1,1024,128]{2,1,0:T(8,128)S(1)}, s32[16]{0:T(128)S(1)}, /*index=5...) while((s32[]{:T(128)}, f32[1,1024]{1,0:T(1,128)S(1)}, ...), condition=%wide.region_11.12_spmd.clone, body=%wide.region_8.11_spmd.clone.sunk | while | flops 280377856 | bytes 7966885 | solution.py:137
  208.8 6.2 %gather_fusion.3 = bf16[2048,128]{1,0:T(8,128)(2,1)S(1)} fusion(bf16[1024,128]{1,0:T(8,128)(2,1)S(1)} %fusion.51, s32[2048]{0:T(1024)S(1)} %get-tuple-element.169), kind=kCustom, calls=%fused_computation.3 | custom fusion | bytes 1056768 | tf_op jit(solution)/shard_map/gather | solution.py:144
  215.0 4.6 fusion.48
  219.6 7.1 %bitcast_multiply_fusion = f32[2048,2048]{1,0:T(8,128)} fusion(f32[8,256,2048]{2,1,0:T(8,128)S(1)} %fusion.48, f32[2048]{0:T(1024)S(1)} %scatter_custom_fusion.2), kind=kLoop, calls=%fused_computation.55 | loop fusion | flops 4194304 | bytes 33562624 | tf_op jit(solution)/shard_map/mul | solution.py:153
  226.7 29.5 %scatter_custom_fusion.3 = f32[512,2048]{1,0:T(8,128)} fusion(s32[2048]{0:T(1024)S(1)} %get-tuple-element.164, f32[2048,2048]{1,0:T(8,128)} %bitcast_multiply_fusion, f32[]{:T(128)} %constant.102.clone.1), kind=kCustom, calls=%fused_computation.66 | custom fusion | flops 4194304 | bytes 4194816 | tf_op jit(solution)/shard_map/scatter-add | solution.py:153
  256.1 2.5 convert_element_type.51
  258.7 2.5 copy.41
  264.3 5.5 %all-to-all-start = ((s32[16,1,2]{2,1,0:T(1,128)}), s32[16,1,2]{2,1,0:T(1,128)S(1)}, u32[]{:S(2)}, u32[]{:S(2)}) async-start(s32[16,1,2]{2,1,0:T(1,128)} %bitcast.16), calls=%async_computation | async-start | bytes 16384 | tf_op jit(solution)/shard_map/all_to_all | solution.py:46
  271.1 2.4 all-to-all-done
  273.5 5.7 %all-to-all-start.1 = ((bf16[16,2,16,2,128]{4,2,3,1,0:T(8,128)(2,1)}), bf16[16,2,16,2,128]{4,2,3,1,0:T(8,128)(2,1)S(1)}, u32[]{:S(2)}, u32[]{:S(2)}) async-start(bf16[16,2,16,2,128]{4,2,3,1,0:T(8,128)(2,1)} %bitcast.19), calls=%async_computation.1 | async-start | bytes 524288 | tf_op jit(solution)/shard_map/all_to_all | solution.py:45
  279.4 4.8 %all-to-all-done.1 = bf16[16,2,16,2,128]{4,2,3,1,0:T(8,128)(2,1)S(1)} async-done(((bf16[16,2,16,2,128]{4,2,3,1,0:T(8,128)(2,1)}), bf16[16,2,16,2,128]{4,2,3,1,0:T(8,128)(2,1)S(1)}, u32[]{:S(2)}, u32[]{:S(2)}) %all-to-all-start.1) | async-done | bytes 262176 | tf_op jit(solution)/shard_map/all_to_all | solution.py:45
  286.7 180.0 %reduce-scatter.4.cloned.1.call-done = bf16[128,512]{1,0:T(8,128)(2,1)} async-done(((bf16[2048,512]{1,0:T(8,128)(2,1)}), bf16[128,512]{1,0:T(8,128)(2,1)}) %reduce-scatter.4.cloned.1.call-update) | async-done | bytes 131088
  (228 shorter events, 91.2 us)
Async XLA Ops:
  7.2 65.0 %copy-start = (f32[2048,8]{0,1:T(8,128)S(1)}, f32[2048,8]{0,1:T(8,128)}, u32[]{:S(2)}) copy-start(f32[2048,8]{0,1:T(8,128)} %param.15) | copy-start | bytes 196612
  7.2 3.8 copy-start.7
  7.2 39.6 %all-gather.5.cloned.1.call-start = ((), (), s32[]{:S(2)}) async-start(), calls=%async_computation.3 | async-start | bytes 1114112 | tf_op jit(solution)/shard_map/all_gather | solution.py:87
  7.9 82.1 %all-gather.9.cloned.1.call-start = ((), (), s32[]{:S(2)}) async-start(), calls=%async_computation.5 | async-start | bytes 4456448 | tf_op jit(solution)/shard_map/all_gather | solution.py:86
  8.7 122.4 %all-gather.7.cloned.1.call-start = ((), (), s32[]{:S(2)}) async-start(), calls=%async_computation.4 | async-start | bytes 4456448 | tf_op jit(solution)/shard_map/all_gather | solution.py:109
  8.7 2.3 copy-start.4
  11.5 38.6 %copy-start.6 = (s32[512,2]{0,1:T(2,128)S(1)}, s32[512,2]{0,1:T(2,128)}, u32[]{:S(2)}) copy-start(s32[512,2]{0,1:T(2,128)} %param.13) | copy-start | bytes 12292
  11.5 39.1 %copy-start.2 = (s32[8192]{0:T(1024)S(1)}, s32[8192]{0:T(1024)}, u32[]{:S(2)}) copy-start(s32[8192]{0:T(1024)} %param.12) | copy-start | bytes 98308
  49.4 165.5 %all-gather.11.cloned.1.call-start = ((), (), s32[]{:S(2)}) async-start(), calls=%async_computation.6 | async-start | bytes 4456448 | tf_op jit(solution)/shard_map/all_gather | solution.py:147
  50.0 416.7 %reduce-scatter.4.cloned.1.call-start = ((), (), s32[]{:S(2)}) async-start(), calls=%async_computation.7 | async-start | bytes 2228224
  261.2 0.7 copy-start.3
  261.2 8.7 %copy-start.5 = (bf16[512,2,128]{2,0,1:T(8,128)(2,1)S(1)}, bf16[512,2,128]{2,0,1:T(8,128)(2,1)}, u32[]{:S(2)}) copy-start(bf16[512,2,128]{2,0,1:T(8,128)(2,1)} %fusion.45) | copy-start | bytes 786436
  261.8 207.6 %copy-start.1 = (f32[2048,8]{0,1:T(8,128)S(1)}, f32[2048,8]{0,1:T(8,128)}, u32[]{:S(2)}) copy-start(f32[2048,8]{0,1:T(8,128)} %param.15) | copy-start | bytes 196612
  264.3 9.3 %all-to-all-start = ((s32[16,1,2]{2,1,0:T(1,128)}), s32[16,1,2]{2,1,0:T(1,128)S(1)}, u32[]{:S(2)}, u32[]{:S(2)}) async-start(s32[16,1,2]{2,1,0:T(1,128)} %bitcast.16), calls=%async_computation | async-start | bytes 16384 | tf_op jit(solution)/shard_map/all_to_all | solution.py:46
  273.5 10.7 %all-to-all-start.1 = ((bf16[16,2,16,2,128]{4,2,3,1,0:T(8,128)(2,1)}), bf16[16,2,16,2,128]{4,2,3,1,0:T(8,128)(2,1)S(1)}, u32[]{:S(2)}, u32[]{:S(2)}) async-start(bf16[16,2,16,2,128]{4,2,3,1,0:T(8,128)(2,1)} %bitcast.19), calls=%async_computation.1 | async-start | bytes 524288 | tf_op jit(solution)/shard_map/all_to_all | solution.py:45
Sparse Core Ops, SparseCore 0:
  9.8 36.9 all-gather.4
  48.6 40.0 all-gather.8
  91.0 40.0 all-gather.6
  132.7 49.4 all-gather.10
  261.3 205.3 reduce-scatter.3
where the time goes:
time: 477 us; the launch traced here: 476 us
  waiting for transfers between devices  255 us (53%)
  other arithmetic  69.7 us (15%)
  local copies, waits for them, and re-layouts  67.9 us (14%)
  matrix products  56.2 us (12%)
  between operations  14.2 us (3%)
  starting transfers between devices  11.4 us (2%)
    unnamed x6, waiting for transfers between devices  182 us
    all_gather x1, waiting for transfers between devices, local(): key_part = lax.all_gather(kv_weight, 'tok', axis=1, tiled=True)  35.2 us
    all_gather x1, waiting for transfers between devices, local(): piece = lax.all_gather(key_values, 'tok', axis=0, tiled=True)  30.9 us
    scatter-add x1, other arithmetic, local(): jnp.zeros((tok_dev, count), jnp.float32).at[slot_token]  29.5 us
    dot_general x16, matrix products, one_block(): jnp.einsum('hqd,khd->hqk', by_head_q, key_block, preferred_element_type=j...  24.3 us
    dot_general x16, matrix products, one_block(): jnp.einsum('hqk,khd->hqd', expon.astype(jnp.bfloat16), value_block, prefe...  16 us
    reduce_sum x16, other arithmetic, one_block(): total = total * shrink + jnp.sum(expon, axis=-1)  12.1 us
    gather x1, local copies, waits for them, and re-layouts, local(): normed[slot_token] * slot_filled[:, None]  11 us
  transfers between devices with their start and end apart: 7, of which 5 were waited for; matrix products, arithmetic and copies ran while one was open for 30% of the time, Pallas kernels for 0%

commit v1 on v0

--- a/solution.py
+++ b/solution.py
@@ -83,8 +83,10 @@
     slot_filled = jnp.zeros((experts * capacity,), jnp.bfloat16).at[slots].set(jnp.bfloat16(1.0))
     slot_gate = jnp.zeros((experts * capacity,), jnp.float32).at[slots].set(gates.reshape(-1))
     grouped = (normed[slot_token] * slot_filled[:, None]).reshape(experts, capacity, width)
-    query_part = lax.all_gather(query_weight, "tok", axis=1, tiled=True)
-    key_part = lax.all_gather(kv_weight, "tok", axis=1, tiled=True)
+    reached = jax.lax.all_gather(
+        jnp.concatenate([query_weight, kv_weight], axis=0), "tok", tiled=True, axis=1
+    )
+    query_part, key_part = jnp.split(reached, [query_weight.shape[0]], axis=0)
     query_total = jnp.einsum(
         "ecd,edh->ech", grouped, query_part, preferred_element_type=jnp.float32
     )

time: 477 us -> 452 us (0.948)
  waiting for transfers between devices: 255 us -> 230 us
    all_gather x1, waiting for transfers between devices: 30.9 us -> 0.02 us  [local(): piece = lax.all_gather(key_values, 'tok', axis=0, tiled=True)]
    all_gather x2 -> x1, waiting for transfers between devices: 35.2 us -> 41.6 us  [local(): jax.lax.all_gather(jnp.concatenate([query_weight, kv_weight], axis=0), 't...]
    unnamed x6 -> x5, waiting for transfers between devices: 182 us -> 181 us
  transfers between devices with their start and end apart: 7 -> 6, of which waited for: 5 -> 4; matrix products, arithmetic and copies ran while one was open for 30% -> 31% of each run, Pallas kernels for 0% -> 0%
where the time goes in v1:
time: 452 us; the launch traced here: 451 us
  waiting for transfers between devices  230 us (51%)
  other arithmetic  70.5 us (16%)
  local copies, waits for them, and re-layouts  67.8 us (15%)
  matrix products  56.2 us (12%)
  between operations  14.2 us (3%)
  starting transfers between devices  10.9 us (2%)
    unnamed x5, waiting for transfers between devices  181 us
    all_gather x1, waiting for transfers between devices, local(): jax.lax.all_gather(jnp.concatenate([query_weight, kv_weight], axis=0), 't...  41.6 us
    scatter-add x1, other arithmetic, local(): jnp.zeros((tok_dev, count), jnp.float32).at[slot_token]  29.5 us
    dot_general x16, matrix products, one_block(): jnp.einsum('hqd,khd->hqk', by_head_q, key_block, preferred_element_type=j...  24.3 us
    dot_general x16, matrix products, one_block(): jnp.einsum('hqk,khd->hqd', expon.astype(jnp.bfloat16), value_block, prefe...  16 us
    reduce_sum x16, other arithmetic, one_block(): total = total * shrink + jnp.sum(expon, axis=-1)  12.1 us
    gather x1, local copies, waits for them, and re-layouts, local(): normed[slot_token] * slot_filled[:, None]  11 us
    dynamic_slice x16, local copies, waits for them, and re-layouts, local(): state, _ = lax.scan(one_block, state, (key_blocks, value_blocks, firsts))  9.42 us
  transfers between devices with their start and end apart: 6, of which 4 were waited for; matrix products, arithmetic and copies ran while one was open for 31% of the time, Pallas kernels for 0%

profile of v1, /device:TPU:4, one launch (start us, length us, event | category | flops | bytes accessed | tf_op | source)
XLA Modules:
  0.0 450.9 jit_solution(4743075321639211674)
XLA Ops:
  9.1 2.2 fusion.34
  11.9 41.6 %all-gather.4.cloned.1.call-done = bf16[10,2048,128]{2,1,0:T(8,128)(2,1)} async-done(((bf16[10,128,128]{2,1,0:T(8,128)(2,1)}), bf16[10,2048,128]{2,1,0:T(8,128)(2,1)}) %all-gather.4.cloned.1.call-update) | async-done | bytes 5242896 | tf_op jit(solution)/shard_map/all_gather | solution.py:86
  53.5 2.6 fusion.48
  57.7 6.2 %gather_fusion = s32[1024]{0:T(1024)S(1)} fusion(s32[8192]{0:T(1024)S(1)} %copy-done.2, s32[1024]{0:T(1024)S(1)} %broadcast_clamp_fusion.2), kind=kCustom, calls=%fused_computation | custom fusion | bytes 12288 | tf_op jit(solution)/shard_map/gather | solution.py:99
  64.2 2.3 reduce-window.6
  67.1 7.6 %scatter_custom_fusion.1 = bf16[2048]{0:T(1024)(128)(2,1)S(1)} fusion(s32[1024]{0:T(1024)S(1)} %bitcast.129, bf16[1024]{0:T(1024)(128)(2,1)S(1)} %broadcast.244, bf16[]{:T(256)} %constant.112.clone.1), kind=kCustom, calls=%fused_computation.128 | custom fusion | bytes 4098 | tf_op jit(solution)/shard_map/scatter | solution.py:83
  74.7 4.3 scatter_custom_fusion
  81.3 11.0 %gather_fusion.1 = bf16[2048,2048]{1,0:T(8,128)(2,1)} fusion(bf16[512,2048]{1,0:T(8,128)(2,1)S(1)} %fusion.36, s32[2048]{0:T(1024)S(1)} %get-tuple-element.163), kind=kCustom, calls=%fused_computation.1 | custom fusion | bytes 16785408 | tf_op jit(solution)/shard_map/gather | solution.py:85
  92.3 4.5 scatter_custom_fusion.2
  96.8 7.0 %fusion.43 = bf16[8,256,128]{2,1,0:T(8,128)(2,1)S(1)} fusion(bf16[10,2048,128]{2,1,0:T(8,128)(2,1)} %all-gather.4.cloned.1.call-done, bf16[8,256,2048]{2,1,0:T(8,128)(2,1)} %bitcast.111, bf16[8,256]{1,0:T(8,128)(2,1)S(1)} %mul.112), kind=kOutput, calls=%fused_computation.69 | convolution fusion | flops 1078198272 | bytes 13111296 | tf_op jit(solution)/shard_map/ecd,edh->ech/dot_general | solution.py:90
  103.8 3.2 gather_fusion.2
  107.1 3.8 fusion.75
  110.9 72.7 %while.15 = (s32[]{:T(128)}, f32[1,1024]{1,0:T(1,128)S(1)}, f32[1,1024]{1,0:T(1,128)S(1)}, f32[1,1024,128]{2,1,0:T(8,128)S(1)}, s32[16]{0:T(128)S(1)}, /*index=5...) while((s32[]{:T(128)}, f32[1,1024]{1,0:T(1,128)S(1)}, ...), condition=%wide.region_11.12_spmd.clone, body=%wide.region_8.11_spmd.clone.sunk | while | flops 280377856 | bytes 7966885 | solution.py:139
  183.8 6.2 %gather_fusion.3 = bf16[2048,128]{1,0:T(8,128)(2,1)S(1)} fusion(bf16[1024,128]{1,0:T(8,128)(2,1)S(1)} %fusion.55, s32[2048]{0:T(1024)S(1)} %get-tuple-element.169), kind=kCustom, calls=%fused_computation.3 | custom fusion | bytes 1056768 | tf_op jit(solution)/shard_map/gather | solution.py:146
  190.0 4.6 %fusion.52 = f32[8,256,2048]{2,1,0:T(8,128)S(1)} fusion(bf16[8,128,2048]{2,1,0:T(8,128)(2,1)} %all-gather.8.cloned.1.call-done, bf16[8,256,128]{2,1,0:T(8,128)(2,1)S(1)} %bitcast.114, bf16[8,256]{1,0:T(8,128)(2,1)S(1)} %mul.112), kind=kOutput, calls=%fused_computation.72 | convolution fusion | flops 1074003968 | bytes 21499904 | tf_op jit(solution)/shard_map/ech,ehn->ecn/dot_general | solution.py:151
  194.6 7.1 %bitcast_multiply_fusion = f32[2048,2048]{1,0:T(8,128)} fusion(f32[8,256,2048]{2,1,0:T(8,128)S(1)} %fusion.52, f32[2048]{0:T(1024)S(1)} %scatter_custom_fusion.2), kind=kLoop, calls=%fused_computation.55 | loop fusion | flops 4194304 | bytes 33562624 | tf_op jit(solution)/shard_map/mul | solution.py:155
  201.7 29.5 %scatter_custom_fusion.3 = f32[512,2048]{1,0:T(8,128)} fusion(s32[2048]{0:T(1024)S(1)} %get-tuple-element.164, f32[2048,2048]{1,0:T(8,128)} %bitcast_multiply_fusion, f32[]{:T(128)} %constant.102.clone.1), kind=kCustom, calls=%fused_computation.67 | custom fusion | flops 4194304 | bytes 4194816 | tf_op jit(solution)/shard_map/scatter-add | solution.py:155
  231.2 2.5 convert_element_type.51
  233.7 2.5 copy.41
  239.3 5.1 %all-to-all-start = ((s32[16,1,2]{2,1,0:T(1,128)}), s32[16,1,2]{2,1,0:T(1,128)S(1)}, u32[]{:S(2)}, u32[]{:S(2)}) async-start(s32[16,1,2]{2,1,0:T(1,128)} %bitcast.16), calls=%async_computation | async-start | bytes 16384 | tf_op jit(solution)/shard_map/all_to_all | solution.py:46
  245.7 2.4 all-to-all-done
  248.1 5.7 %all-to-all-start.1 = ((bf16[16,2,16,2,128]{4,2,3,1,0:T(8,128)(2,1)}), bf16[16,2,16,2,128]{4,2,3,1,0:T(8,128)(2,1)S(1)}, u32[]{:S(2)}, u32[]{:S(2)}) async-start(bf16[16,2,16,2,128]{4,2,3,1,0:T(8,128)(2,1)} %bitcast.19), calls=%async_computation.1 | async-start | bytes 524288 | tf_op jit(solution)/shard_map/all_to_all | solution.py:45
  253.9 4.8 %all-to-all-done.1 = bf16[16,2,16,2,128]{4,2,3,1,0:T(8,128)(2,1)S(1)} async-done(((bf16[16,2,16,2,128]{4,2,3,1,0:T(8,128)(2,1)}), bf16[16,2,16,2,128]{4,2,3,1,0:T(8,128)(2,1)S(1)}, u32[]{:S(2)}, u32[]{:S(2)}) %all-to-all-start.1) | async-done | bytes 262176 | tf_op jit(solution)/shard_map/all_to_all | solution.py:45
  261.3 180.4 %reduce-scatter.4.cloned.1.call-done = bf16[128,512]{1,0:T(8,128)(2,1)} async-done(((bf16[2048,512]{1,0:T(8,128)(2,1)}), bf16[128,512]{1,0:T(8,128)(2,1)}) %reduce-scatter.4.cloned.1.call-update) | async-done | bytes 131088
  (226 shorter events, 88.5 us)
Async XLA Ops:
  7.2 71.9 %copy-start = (f32[2048,8]{0,1:T(8,128)S(1)}, f32[2048,8]{0,1:T(8,128)}, u32[]{:S(2)}) copy-start(f32[2048,8]{0,1:T(8,128)} %param.15) | copy-start | bytes 196612
  7.2 4.1 copy-start.7
  7.2 46.3 %all-gather.4.cloned.1.call-start = ((), (), s32[]{:S(2)}) async-start(), calls=%async_computation.3 | async-start | bytes 5570560 | tf_op jit(solution)/shard_map/all_gather | solution.py:86
  9.0 98.1 %all-gather.6.cloned.1.call-start = ((), (), s32[]{:S(2)}) async-start(), calls=%async_computation.4 | async-start | bytes 4456448 | tf_op jit(solution)/shard_map/all_gather | solution.py:111
  9.0 2.3 copy-start.4
  11.9 45.1 %copy-start.6 = (s32[512,2]{0,1:T(2,128)S(1)}, s32[512,2]{0,1:T(2,128)}, u32[]{:S(2)}) copy-start(s32[512,2]{0,1:T(2,128)} %param.13) | copy-start | bytes 12292
  11.9 45.6 %copy-start.2 = (s32[8192]{0:T(1024)S(1)}, s32[8192]{0:T(1024)}, u32[]{:S(2)}) copy-start(s32[8192]{0:T(1024)} %param.12) | copy-start | bytes 98308
  56.2 133.8 %all-gather.8.cloned.1.call-start = ((), (), s32[]{:S(2)}) async-start(), calls=%async_computation.5 | async-start | bytes 4456448 | tf_op jit(solution)/shard_map/all_gather | solution.py:149
  56.9 384.8 %reduce-scatter.4.cloned.1.call-start = ((), (), s32[]{:S(2)}) async-start(), calls=%async_computation.6 | async-start | bytes 2228224
  236.2 0.7 copy-start.3
  236.2 8.2 %copy-start.5 = (bf16[512,2,128]{2,0,1:T(8,128)(2,1)S(1)}, bf16[512,2,128]{2,0,1:T(8,128)(2,1)}, u32[]{:S(2)}) copy-start(bf16[512,2,128]{2,0,1:T(8,128)(2,1)} %fusion.48) | copy-start | bytes 786436
  236.9 207.5 %copy-start.1 = (f32[2048,8]{0,1:T(8,128)S(1)}, f32[2048,8]{0,1:T(8,128)}, u32[]{:S(2)}) copy-start(f32[2048,8]{0,1:T(8,128)} %param.15) | copy-start | bytes 196612
  239.3 8.8 %all-to-all-start = ((s32[16,1,2]{2,1,0:T(1,128)}), s32[16,1,2]{2,1,0:T(1,128)S(1)}, u32[]{:S(2)}, u32[]{:S(2)}) async-start(s32[16,1,2]{2,1,0:T(1,128)} %bitcast.16), calls=%async_computation | async-start | bytes 16384 | tf_op jit(solution)/shard_map/all_to_all | solution.py:46
  248.1 10.7 %all-to-all-start.1 = ((bf16[16,2,16,2,128]{4,2,3,1,0:T(8,128)(2,1)}), bf16[16,2,16,2,128]{4,2,3,1,0:T(8,128)(2,1)S(1)}, u32[]{:S(2)}, u32[]{:S(2)}) async-start(bf16[16,2,16,2,128]{4,2,3,1,0:T(8,128)(2,1)} %bitcast.19), calls=%async_computation.1 | async-start | bytes 524288 | tf_op jit(solution)/shard_map/all_to_all | solution.py:45
Sparse Core Ops, SparseCore 0:
  9.8 43.6 all-gather.3
  56.3 40.2 all-gather.5
  98.3 49.4 all-gather.7
  236.4 205.3 reduce-scatter.3
